TPU v7x, 256 devices: a whole 4x4x8 slice. The times are simulated.
256 devices in a mesh: det: 64 (over z, y, core), tm: 4 (over x).
Axes of the slice: x: 4, y: 4, z: 8, core: 2. Of those that a mesh axis runs over, the one named last changes fastest.
Arguments:
- time_streams: float32 [64, 1, 4096], P('det', None, 'tm'), may hold values from -12 to 12
- pol_angle: float32 [64, 1, 4096], P('det', None, 'tm'), may hold values from -3.140625 to 3.140625
- offsets: int32 [64, 1, 4096], P('det', None, 'tm'), may hold values from 0 to 255
- block_slots: int32 [64, 1, 16], P('det', None, 'tm'), may hold values from 0 to 127
- hit_ids: int32 [64, 128], P('det'), may hold values from 0 to 1023, as said below
- valid_counts: int32 [64, 1], P('det'), may hold values from 1024 to 4096
- filter_taps: float32 [64, 1, 65], P('det'), may hold values from -0.75 to 0.75
- white_weight: float32 [64, 1], P('det'), may hold values from 0.5 to 2
Outputs:
- solution_map: float32 [1024, 3, 256], P('det')
- precond_residual: float32 [1024, 3, 256], P('det')
Inputs may be any that keep to these rules, and one draw needn't show every extreme that they name: `hit_ids`: slot o * 2 + c of a section names a block of o * 16 .. (o + 1) * 16 - 1, and the 2 blocks of one o in one section differ.
All inputs are finite; a program needn't handle non-finite values.
Results may differ from a plain program's by a relative error of at most 0.0003.
Values sent between devices are 32-bit elements; how exact they have to be, the bound alone decides.
A program may use at most 128 MiB of HBM per device.

v0:
```python
import jax
import jax.numpy as jnp
from jax import lax
from jax.sharding import PartitionSpec as P

BLK = 256
WIN = 256
BAND = 64
ITERS = 2
NDET = 1
TCH = 1024
BPD = 16
CAP = 2
highest = lax.Precision.HIGHEST


def with_halo(cells, sides, width):
    for axis, dim in sides:
        count = lax.axis_size(axis)
        ends = count - 1
        head = lax.slice_in_dim(cells, 0, width, axis=dim)
        tail = lax.slice_in_dim(cells, cells.shape[dim] - width, cells.shape[dim], axis=dim)
        cells = jnp.concatenate(
            [
                lax.ppermute(tail, axis, [(i, (i + 1) % count) for i in range(ends)]),
                cells,
                lax.ppermute(head, axis, [((i + 1) % count, i) for i in range(ends)]),
            ],
            axis=dim,
        )
    return cells


def lag_table(filter_taps, white_weight):
    columns = []
    for shift_lag in range(BAND + 1):
        columns.append(
            jnp.sum(
                filter_taps[..., : BAND + 1 - shift_lag] * filter_taps[..., shift_lag:], axis=-1
            )
        )
    lags = jnp.stack(columns, axis=-1)
    return lags.at[..., 0].add(white_weight)


def toeplitz_matrix(lags):
    row_index = jnp.arange(WIN + 2 * BAND, dtype=jnp.int32)[:, None]
    col_index = jnp.arange(WIN, dtype=jnp.int32)[None, :]
    distance = jnp.abs(row_index - BAND - col_index)
    inside = distance <= BAND
    clipped = jnp.minimum(distance, BAND)
    return jnp.where(inside[None], lags[:, clipped], 0.0)


def precondition(weights, residual):
    entry_aa = 1.0 + weights[:, 0]
    entry_ab = weights[:, 1]
    entry_ac = weights[:, 2]
    entry_bb = 1.0 + weights[:, 3]
    entry_bc = weights[:, 4]
    entry_cc = 1.0 + weights[:, 5]
    minor_aa = entry_bb * entry_cc - entry_bc * entry_bc
    minor_ab = entry_ac * entry_bc - entry_ab * entry_cc
    minor_ac = entry_ab * entry_bc - entry_ac * entry_bb
    minor_bb = entry_aa * entry_cc - entry_ac * entry_ac
    minor_bc = entry_ab * entry_ac - entry_aa * entry_bc
    minor_cc = entry_aa * entry_bb - entry_ab * entry_ab
    determinant = entry_aa * minor_aa + entry_ab * minor_ab + entry_ac * minor_ac
    stokes_i = residual[:, 0]
    stokes_q = residual[:, 1]
    stokes_u = residual[:, 2]
    return jnp.stack(
        [
            (minor_aa * stokes_i + minor_ab * stokes_q + minor_ac * stokes_u) / determinant,
            (minor_ab * stokes_i + minor_bb * stokes_q + minor_bc * stokes_u) / determinant,
            (minor_ac * stokes_i + minor_bc * stokes_q + minor_cc * stokes_u) / determinant,
        ],
        axis=1,
    )


def global_dot(left, right):
    return lax.psum(jnp.sum(left * right), "det")


def per_device(
    time_streams, pol_angle, offsets, block_slots, hit_ids, valid_counts, filter_taps, white_weight
):
    det_count = lax.axis_size("det")
    block_count = TCH // WIN
    lags = lag_table(filter_taps[0], white_weight[0])
    matrix = toeplitz_matrix(lags)
    hit_row = hit_ids[0]
    hit_total = hit_row.shape[0]
    span_start = lax.axis_index("tm") * TCH
    sample_time = span_start + jnp.arange(TCH, dtype=jnp.int32)
    live_mask = (
        (sample_time[None, :] < valid_counts[0][:, None])
        .astype(jnp.float32)
        .reshape(NDET, block_count, WIN)
    )
    cosine = jnp.cos(2.0 * pol_angle[0]).reshape(NDET, block_count, WIN)
    sine_term = jnp.sin(2.0 * pol_angle[0]).reshape(NDET, block_count, WIN)
    pixel_pick = (
        offsets[0].reshape(NDET, block_count, WIN, 1) == jnp.arange(BLK, dtype=jnp.int32)
    ).astype(jnp.float32)
    slot_pick = (jnp.arange(hit_total, dtype=jnp.int32)[:, None] == block_slots[0]).astype(
        jnp.float32
    )
    place_pick = (
        (hit_row.reshape(det_count, CAP) % BPD)[:, :, None] == jnp.arange(BPD, dtype=jnp.int32)
    ).astype(jnp.float32)

    def noise_filter(signal):
        padded = with_halo(signal.reshape(NDET, TCH), (("tm", 1),), BAND)
        extended = jnp.pad(padded, ((0, 0), (0, WIN - 2 * BAND)))
        leading = extended[:, :TCH].reshape(NDET, block_count, WIN)
        trailing = extended[:, WIN : WIN + TCH].reshape(NDET, block_count, WIN)[:, :, : 2 * BAND]
        window = jnp.concatenate([leading, trailing], axis=2)
        return jnp.einsum("djo,dok->djk", window, matrix, precision=highest)

    def bin_samples(components):
        comp_count = components.shape[2]
        per_block = jnp.einsum("djwp,djkw->djkp", pixel_pick, components, precision=highest)
        summed = jnp.dot(
            slot_pick, per_block.reshape(NDET * block_count, comp_count * BLK), precision=highest
        )
        return summed.reshape(hit_total, comp_count, BLK)

    def to_owner_blocks(binned):
        comp_count = binned.shape[1]
        pixel_part = binned.shape[2]
        grouped = binned.reshape(det_count, CAP, comp_count * pixel_part)
        whole_map = jnp.einsum("ocb,ocx->obx", place_pick, grouped, precision=highest)
        whole_map = whole_map.reshape(det_count * BPD, comp_count, pixel_part)
        owned_map = lax.psum_scatter(whole_map, "det", scatter_dimension=0, tiled=True)
        owned_map = lax.psum(owned_map, "tm")
        return owned_map

    filtered = noise_filter(time_streams[0].reshape(NDET, block_count, WIN) * live_mask) * live_mask
    weight = lags[:, 0][:, None, None] * live_mask
    components = jnp.stack(
        [
            filtered,
            filtered * cosine,
            filtered * sine_term,
            weight,
            weight * cosine,
            weight * sine_term,
            weight * cosine * cosine,
            weight * cosine * sine_term,
            weight * sine_term * sine_term,
        ],
        axis=2,
    )
    initial = to_owner_blocks(bin_samples(components))
    right_side = initial[:, :3]
    weights = initial[:, 3:]
    solution = jnp.zeros_like(right_side)
    residual = right_side
    descent = precondition(weights, residual)
    direction = descent
    product_now = global_dot(residual, descent)
    for iteration in range(ITERS):
        from_whole_map = lax.all_gather(direction, "det", axis=0, tiled=True)
        from_grouped = from_whole_map.reshape(det_count, BPD, 3 * BLK)
        picked = jnp.einsum("ocb,obx->ocx", place_pick, from_grouped, precision=highest)
        fetched = picked.reshape(hit_total, 3, BLK)
        apply_per_block = jnp.dot(
            slot_pick.T, fetched.reshape(hit_total, 3 * BLK), precision=highest
        )
        apply_per_block = apply_per_block.reshape(NDET, block_count, 3, BLK)
        values = jnp.einsum("djwp,djcp->djcw", pixel_pick, apply_per_block, precision=highest)
        apply_signal = (
            values[:, :, 0] + values[:, :, 1] * cosine + values[:, :, 2] * sine_term
        ) * live_mask
        apply_filtered = noise_filter(apply_signal) * live_mask
        apply_components = jnp.stack(
            [apply_filtered, apply_filtered * cosine, apply_filtered * sine_term], axis=2
        )
        image_map = to_owner_blocks(bin_samples(apply_components))
        step_size = product_now / global_dot(direction, image_map)
        solution = solution + step_size * direction
        residual = residual - step_size * image_map
        descent = precondition(weights, residual)
        if iteration + 1 < ITERS:
            product_next = global_dot(residual, descent)
            direction = descent + product_next / product_now * direction
            product_now = product_next
    return (solution, descent)


def solution(mesh):
    in_specs = (
        P("det", None, "tm"),
        P("det", None, "tm"),
        P("det", None, "tm"),
        P("det", None, "tm"),
        P("det", None),
        P("det", None),
        P("det", None, None),
        P("det", None),
    )
    out_specs = (P("det", None, None), P("det", None, None))
    return jax.shard_map(
        per_device, mesh=mesh, in_specs=in_specs, out_specs=out_specs, check_vma=False
    )
```

profile of v0, /device:TPU:1, one launch (start us, length us, event | category | flops | bytes accessed | tf_op | source)
XLA Modules:
  0.0 1986.2 jit_solution(1493701683084729770)
XLA Ops:
  8.6 3.9 collective-permute-start
  48.3 1.5 multiply_reduce_fusion.39
  57.0 1.5 multiply_reduce_fusion.33
  113.4 583.8 %gather_fusion = f32[98304]{0:T(1024)S(1)} fusion(f32[65]{0:T(128)S(1)} %bitcast_dynamic-update-slice_fusion, s32[98304]{0:T(1024)S(1)} %broadcast_clamp_fusion), kind=kCustom, calls=%fused_computation | custom fusion | bytes 1179648 | tf_op jit(solution)/shard_map/gather | solution.py:52
  701.8 7.9 fusion
  709.7 12.7 reshape.851
  722.4 14.9 copy.43
  737.3 156.0 %reduce-scatter.2.cloned.1.call-done = f32[16,9,256]{2,0,1:T(8,128)} async-done(((f32[1024,9,256]{2,0,1:T(8,128)}), f32[16,9,256]{2,0,1:T(8,128)}) %reduce-scatter.2.cloned.1.call-update) | async-done | bytes 147472 | tf_op jit(solution)/shard_map/reduce_scatter | solution.py:136
  893.6 49.2 %all-reduce.10.cloned.1.call-done = f32[16,9,256]{2,0,1:T(8,128)} async-done(((f32[16,9,256]{2,0,1:T(8,128)}), f32[16,9,256]{2,0,1:T(8,128)}) %all-reduce.10.cloned.1.call-update) | async-done | bytes 147472 | tf_op jit(solution)/shard_map/psum | solution.py:137
  948.4 80.5 %all-gather.3.cloned.1.call-done = f32[1024,3,256]{2,0,1:T(8,128)} async-done(((f32[16,3,256]{2,0,1:T(8,128)}), f32[1024,3,256]{2,0,1:T(8,128)}) %all-gather.3.cloned.1.call-update) | async-done | bytes 3145744 | tf_op jit(solution)/shard_map/all_gather | solution.py:165
  1028.9 6.0 copy.44
  1034.9 4.8 reshape.852
  1039.7 2.0 fusion.33
  1045.4 3.1 collective-permute-start.2
  1049.9 2.9 collective-permute-done.3
  1056.8 2.9 fusion.16
  1059.7 3.3 reshape.858
  1064.9 191.2 %all-reduce.12.cloned.1.call-done = f32[1024,3,256]{2,1,0:T(4,128)} async-done(((f32[1024,3,256]{2,1,0:T(4,128)}), f32[1024,3,256]{2,1,0:T(4,128)}) %all-reduce.12.cloned.1.call-update) | async-done | bytes 3145744
  1257.0 13.5 psum.51
  1271.2 130.2 %all-reduce.5 = (f32[]{:T(128)}, f32[]{:T(128)}) all-reduce(f32[]{:T(128)} %get-tuple-element.19, f32[]{:T(128)} %get-tuple-element.18), channel_id=1, replica_groups=mesh['det'=64,'tm'=4] {'det'}, use_global_device_ids=true, to_apply=%region_68.69 | all-reduce | flops 2 | bytes 16 | tf_op jit(solution)/shard_map/psum | solution.py:83
  1404.0 124.6 %psum.53 = f32[]{:T(128)} all-reduce(f32[]{:T(128)} %multiply_reduce_fusion.1), channel_id=1, replica_groups=mesh['det'=64,'tm'=4] {'det'}, use_global_device_ids=true, to_apply=%region_74.75 | all-reduce | flops 1 | bytes 8 | tf_op jit(solution)/shard_map/psum | solution.py:83
  1530.8 73.7 %all-gather.5.cloned.1.call-done = f32[1024,3,256]{2,0,1:T(8,128)} async-done(((f32[16,3,256]{2,0,1:T(8,128)}), f32[1024,3,256]{2,0,1:T(8,128)}) %all-gather.5.cloned.1.call-update) | async-done | bytes 3145744 | tf_op jit(solution)/shard_map/all_gather | solution.py:165
  1604.5 6.0 copy.50
  1610.5 4.8 reshape.859
  1615.3 2.0 fusion.32
  1621.0 3.1 collective-permute-start.4
  1625.6 2.9 collective-permute-done.5
  1632.4 2.9 fusion.14
  1635.3 3.3 reshape.865
  1638.7 192.7 %all-reduce.14.cloned.1.call-done = f32[1024,3,256]{2,1,0:T(4,128)} async-done(((f32[1024,3,256]{2,1,0:T(4,128)}), f32[1024,3,256]{2,1,0:T(4,128)}) %all-reduce.14.cloned.1.call-update) | async-done | bytes 3145744
  1832.3 13.5 psum.54
  1846.5 130.2 %psum.55 = f32[]{:T(128)} all-reduce(f32[]{:T(128)} %multiply_reduce_fusion), channel_id=1, replica_groups=mesh['det'=64,'tm'=4] {'det'}, use_global_device_ids=true, to_apply=%region_78.79 | all-reduce | flops 1 | bytes 8 | tf_op jit(solution)/shard_map/psum | solution.py:83
  (276 shorter events, 130.4 us)
Async XLA Ops:
  7.2 886.2 %reduce-scatter.2.cloned.1.call-start = ((), (), s32[]{:S(2)}) async-start(), calls=%async_computation.1 | async-start | bytes 9584640 | tf_op jit(solution)/shard_map/reduce_scatter | solution.py:136
  8.6 691.0 %collective-permute-start = (f32[1,64]{1,0:T(1,128)S(1)}, f32[1,64]{1,0:T(1,128)S(1)}, u32[]{:S(2)}, u32[]{:S(2)}) collective-permute-start(f32[1,64]{1,0:T(1,128)S(1)} %get-tuple-element.57), channel_id=1, source_target_pairs={{0,1},{1,2},{2,3},{4,5},{5,6},{6,7},{8,9},{9,10},{10,11},{12,13},{... | collective-permute-start | bytes 776 | tf_op jit(solution)/shard_map/ppermute | solution.py:25
  12.6 687.0 %collective-permute-start.1 = (f32[1,64]{1,0:T(1,128)S(1)}, f32[1,64]{1,0:T(1,128)S(1)}, u32[]{:S(2)}, u32[]{:S(2)}) collective-permute-start(f32[1,64]{1,0:T(1,128)S(1)} %get-tuple-element.56), channel_id=1, source_target_pairs={{1,0},{2,1},{3,2},{5,4},{6,5},{7,6},{9,8},{10,9},{11,10},{13,12},{... | collective-permute-start | bytes 776 | tf_op jit(solution)/shard_map/ppermute | solution.py:27
  107.8 592.1 %copy-start.44 = (s32[384]{0:T(512)}, s32[384]{0:T(512)S(1)}, u32[]{:S(2)}) copy-start(s32[384]{0:T(512)S(1)} %iota_add_fusion) | copy-start | bytes 4612
  107.8 593.2 %copy-start.41 = (s32[64,2]{0,1:T(2,128)}, s32[64,2]{0,1:T(2,128)S(1)}, u32[]{:S(2)}) copy-start(s32[64,2]{0,1:T(2,128)S(1)} %multiply_add_fusion.3) | copy-start | bytes 1540
  113.3 584.0 %copy-start.37 = (f32[1,1,1024]{2,1,0:T(1,128)S(1)}, f32[1,1,1024]{2,1,0:T(1,128)}, u32[]{:S(2)}) copy-start(f32[1,1,1024]{2,1,0:T(1,128)} %param.11) | copy-start | bytes 12292
  113.3 584.7 %copy-start.47 = (s32[1,128]{1,0:T(1,128)S(1)}, s32[1,128]{1,0:T(1,128)}, u32[]{:S(2)}) copy-start(s32[1,128]{1,0:T(1,128)} %param.14) | copy-start | bytes 1540
  113.3 585.6 %copy-start.45 = (s32[1,1,1024]{2,1,0:T(1,128)S(1)}, s32[1,1,1024]{2,1,0:T(1,128)}, u32[]{:S(2)}) copy-start(s32[1,1,1024]{2,1,0:T(1,128)} %param.12) | copy-start | bytes 12292
  113.3 587.6 %copy-start.38 = (s32[1,1,4]{2,1,0:T(1,128)S(1)}, s32[1,1,4]{2,1,0:T(1,128)}, u32[]{:S(2)}) copy-start(s32[1,1,4]{2,1,0:T(1,128)} %param.13) | copy-start | bytes 52
  737.3 205.5 %all-reduce.10.cloned.1.call-start = ((), (), s32[]{:S(2)}) async-start(), calls=%async_computation.2 | async-start | bytes 294912 | tf_op jit(solution)/shard_map/psum | solution.py:137
  893.3 135.6 %all-gather.3.cloned.1.call-start = ((), (), s32[]{:S(2)}) async-start(), calls=%async_computation.3 | async-start | bytes 3194880 | tf_op jit(solution)/shard_map/all_gather | solution.py:165
  948.4 307.7 %all-reduce.12.cloned.1.call-start = ((), (), s32[]{:S(2)}) async-start(), calls=%async_computation.5 | async-start | bytes 8388608
  1045.4 4.4 collective-permute-start.2
  1048.5 4.3 collective-permute-start.3
  1063.0 339.8 %copy-start.17 = (f32[16,1,256]{2,0,1:T(8,128)S(1)}, f32[16,1,256]{2,0,1:T(8,128)}, u32[]{:S(2)}) copy-start(f32[16,1,256]{2,0,1:T(8,128)} %copy-done.16) | copy-start | bytes 49156
  1063.0 339.8 %copy-start.21 = (f32[16,1,256]{2,0,1:T(8,128)S(1)}, f32[16,1,256]{2,0,1:T(8,128)}, u32[]{:S(2)}) copy-start(f32[16,1,256]{2,0,1:T(8,128)} %copy-done.20) | copy-start | bytes 49156
  1063.0 339.8 %copy-start.24 = (f32[16,1,256]{2,0,1:T(8,128)S(1)}, f32[16,1,256]{2,0,1:T(8,128)}, u32[]{:S(2)}) copy-start(f32[16,1,256]{2,0,1:T(8,128)} %copy-done.23) | copy-start | bytes 49156
  1063.0 339.8 %copy-start.27 = (f32[16,1,256]{2,0,1:T(8,128)S(1)}, f32[16,1,256]{2,0,1:T(8,128)}, u32[]{:S(2)}) copy-start(f32[16,1,256]{2,0,1:T(8,128)} %copy-done.26) | copy-start | bytes 49156
  1063.0 339.8 %copy-start.29 = (f32[16,1,256]{2,0,1:T(8,128)S(1)}, f32[16,1,256]{2,0,1:T(8,128)}, u32[]{:S(2)}) copy-start(f32[16,1,256]{2,0,1:T(8,128)} %get-tuple-element.26) | copy-start | bytes 49156
  1063.0 339.8 %copy-start.31 = (f32[16,1,256]{2,0,1:T(8,128)S(1)}, f32[16,1,256]{2,0,1:T(8,128)}, u32[]{:S(2)}) copy-start(f32[16,1,256]{2,0,1:T(8,128)} %get-tuple-element.30) | copy-start | bytes 49156
  1063.0 339.8 %copy-start.33 = (f32[16,1,256]{2,0,1:T(8,128)S(1)}, f32[16,1,256]{2,0,1:T(8,128)}, u32[]{:S(2)}) copy-start(f32[16,1,256]{2,0,1:T(8,128)} %get-tuple-element.33) | copy-start | bytes 49156
  1063.1 541.4 %all-gather.5.cloned.1.call-start = ((), (), s32[]{:S(2)}) async-start(), calls=%async_computation.4 | async-start | bytes 3194880 | tf_op jit(solution)/shard_map/all_gather | solution.py:165
  1530.5 300.9 %all-reduce.14.cloned.1.call-start = ((), (), s32[]{:S(2)}) async-start(), calls=%async_computation.6 | async-start | bytes 8388608
  1621.0 4.4 collective-permute-start.4
  1624.1 4.3 collective-permute-start.5
  1638.6 340.1 %copy-start.18 = (f32[16,1,256]{2,0,1:T(8,128)S(1)}, f32[16,1,256]{2,0,1:T(8,128)}, u32[]{:S(2)}) copy-start(f32[16,1,256]{2,0,1:T(8,128)} %copy-done.16) | copy-start | bytes 49156
  1638.6 340.1 %copy-start.22 = (f32[16,1,256]{2,0,1:T(8,128)S(1)}, f32[16,1,256]{2,0,1:T(8,128)}, u32[]{:S(2)}) copy-start(f32[16,1,256]{2,0,1:T(8,128)} %copy-done.20) | copy-start | bytes 49156
  1638.6 340.1 %copy-start.25 = (f32[16,1,256]{2,0,1:T(8,128)S(1)}, f32[16,1,256]{2,0,1:T(8,128)}, u32[]{:S(2)}) copy-start(f32[16,1,256]{2,0,1:T(8,128)} %copy-done.23) | copy-start | bytes 49156
  1638.6 340.0 %copy-start.28 = (f32[16,1,256]{2,0,1:T(8,128)S(1)}, f32[16,1,256]{2,0,1:T(8,128)}, u32[]{:S(2)}) copy-start(f32[16,1,256]{2,0,1:T(8,128)} %copy-done.26) | copy-start | bytes 49156
  1638.6 340.0 %copy-start.30 = (f32[16,1,256]{2,0,1:T(8,128)S(1)}, f32[16,1,256]{2,0,1:T(8,128)}, u32[]{:S(2)}) copy-start(f32[16,1,256]{2,0,1:T(8,128)} %get-tuple-element.26) | copy-start | bytes 49156
  1638.7 340.0 %copy-start.32 = (f32[16,1,256]{2,0,1:T(8,128)S(1)}, f32[16,1,256]{2,0,1:T(8,128)}, u32[]{:S(2)}) copy-start(f32[16,1,256]{2,0,1:T(8,128)} %get-tuple-element.30) | copy-start | bytes 49156
  1638.7 340.0 %copy-start.34 = (f32[16,1,256]{2,0,1:T(8,128)S(1)}, f32[16,1,256]{2,0,1:T(8,128)}, u32[]{:S(2)}) copy-start(f32[16,1,256]{2,0,1:T(8,128)} %get-tuple-element.33) | copy-start | bytes 49156
  (29 other events, 2711.7 us)
Sparse Core Ops, SparseCore 0:
  737.4 155.8 reduce-scatter.1
  895.6 47.0 all-reduce.9
  948.5 80.3 all-gather.2
  1063.2 192.8 all-reduce.11
  1530.7 73.7 all-gather.4
  1638.8 192.5 all-reduce.13
where the time goes:
time: 1990 us
  waiting for transfers between devices  749 us (38%)
  local copies, waits for them, and re-layouts  649 us (33%)
  blocking collectives  412 us (21%)
  other arithmetic  107 us (5%)
  matrix products  30 us (2%)
  between operations  24.3 us (1%)
    gather x2, local copies, waits for them, and re-layouts, toeplitz_matrix(): return jnp.where(inside[None], lags[:, clipped], 0.0)  584 us
    psum x3, blocking collectives, global_dot(): return lax.psum(jnp.sum(left * right), 'det')  385 us
    unnamed x8, waiting for transfers between devices  384 us
    reduce_scatter x1, waiting for transfers between devices, to_owner_blocks(): lax.psum_scatter(whole_map, 'det', scatter_dimension=0, tiled=True)  156 us
    all_gather x2, waiting for transfers between devices, per_device(): from_whole_map = lax.all_gather(direction, 'det', axis=0, tiled=True)  154 us
    reduce_sum x64, other arithmetic, lag_table(): jnp.sum(filter_taps[..., :BAND + 1 - shift_lag] * filter_taps[..., shift_...  91.9 us
    psum x1, waiting for transfers between devices, to_owner_blocks(): owned_map = lax.psum(owned_map, 'tm')  49.2 us
  transfers between devices with their start and end apart: 12, of which 8 were waited for; matrix products, arithmetic and copies ran while one was open for 34% of the time, Pallas kernels for 0%

commit v1 on v0

--- a/solution.py
+++ b/solution.py
@@ -162,7 +162,9 @@
     direction = descent
     product_now = global_dot(residual, descent)
     for iteration in range(ITERS):
-        from_whole_map = lax.all_gather(direction, "det", axis=0, tiled=True)
+        from_whole_map = jnp.concatenate(
+            lax.all_to_all(jnp.stack([direction] * lax.axis_size("det")), "det", 0, 0), axis=0
+        )
         from_grouped = from_whole_map.reshape(det_count, BPD, 3 * BLK)
         picked = jnp.einsum("ocb,obx->ocx", place_pick, from_grouped, precision=highest)
         fetched = picked.reshape(hit_total, 3, BLK)

time: 1990 us -> 1960 us (0.985)
  blocking collectives: 412 us -> 577 us
  waiting for transfers between devices: 749 us -> 593 us
  local copies, waits for them, and re-layouts: 649 us -> 627 us
    all_to_all x0 -> x2, blocking collectives: none -> 165 us  [per_device(): lax.all_to_all(jnp.stack([direction] * lax.axis_size('det')), 'det', 0, 0)]
    all_gather x2 -> x0, waiting for transfers between devices: 154 us -> none  [per_device(): from_whole_map = lax.all_gather(direction, 'det', axis=0, tiled=True)]
    unnamed x8 -> x6, waiting for transfers between devices: 384 us -> 382 us
  transfers between devices with their start and end apart: 12 -> 10, of which waited for: 8 -> 6; matrix products, arithmetic and copies ran while one was open for 34% -> 35% of each run, Pallas kernels for 0% -> 0%
where the time goes in v1:
time: 1960 us; the launch traced here: 1950 us
  local copies, waits for them, and re-layouts  627 us (32%)
  waiting for transfers between devices  593 us (30%)
  blocking collectives  577 us (29%)
  other arithmetic  101 us (5%)
  between operations  23.6 us (1%)
  matrix products  21 us (1%)
    gather x2, local copies, waits for them, and re-layouts, toeplitz_matrix(): return jnp.where(inside[None], lags[:, clipped], 0.0)  584 us
    psum x3, blocking collectives, global_dot(): return lax.psum(jnp.sum(left * right), 'det')  385 us
    unnamed x6, waiting for transfers between devices  382 us
    all_to_all x2, blocking collectives, per_device(): lax.all_to_all(jnp.stack([direction] * lax.axis_size('det')), 'det', 0, 0)  165 us
    reduce_scatter x1, waiting for transfers between devices, to_owner_blocks(): lax.psum_scatter(whole_map, 'det', scatter_dimension=0, tiled=True)  156 us
    reduce_sum x64, other arithmetic, lag_table(): jnp.sum(filter_taps[..., :BAND + 1 - shift_lag] * filter_taps[..., shift_...  91.9 us
    psum x1, waiting for transfers between devices, to_owner_blocks(): owned_map = lax.psum(owned_map, 'tm')  49.2 us
  transfers between devices with their start and end apart: 10, of which 6 were waited for; matrix products, arithmetic and copies ran while one was open for 35% of the time, Pallas kernels for 0%

profile of v1, /device:TPU:1, one launch (start us, length us, event | category | flops | bytes accessed | tf_op | source)
XLA Modules:
  0.0 1955.0 jit_solution(3117108766312398189)
XLA Ops:
  8.6 3.9 collective-permute-start
  20.9 1.5 multiply_reduce_fusion.58
  23.8 1.5 multiply_reduce_fusion.56
  38.2 1.5 multiply_reduce_fusion.46
  39.6 1.5 multiply_reduce_fusion.45
  48.3 1.5 multiply_reduce_fusion.39
  52.6 1.5 multiply_reduce_fusion.36
  57.0 1.5 multiply_reduce_fusion.33
  59.9 1.5 multiply_reduce_fusion.31
  101.5 1.5 multiply_reduce_fusion.65
  113.4 583.8 %gather_fusion = f32[98304]{0:T(1024)S(1)} fusion(f32[65]{0:T(128)S(1)} %bitcast_dynamic-update-slice_fusion, s32[98304]{0:T(1024)S(1)} %broadcast_clamp_fusion), kind=kCustom, calls=%fused_computation | custom fusion | bytes 1179648 | tf_op jit(solution)/shard_map/gather | solution.py:52
  701.7 7.9 fusion
  709.6 12.7 reshape.866
  722.3 14.9 copy.43
  737.2 155.9 %reduce-scatter.2.cloned.1.call-done = f32[16,9,256]{2,0,1:T(8,128)} async-done(((f32[1024,9,256]{2,0,1:T(8,128)}), f32[16,9,256]{2,0,1:T(8,128)}) %reduce-scatter.2.cloned.1.call-update) | async-done | bytes 147472 | tf_op jit(solution)/shard_map/reduce_scatter | solution.py:136
  893.3 49.2 %all-reduce.10.cloned.1.call-done = f32[16,9,256]{2,0,1:T(8,128)} async-done(((f32[16,9,256]{2,0,1:T(8,128)}), f32[16,9,256]{2,0,1:T(8,128)}) %all-reduce.10.cloned.1.call-update) | async-done | bytes 147472 | tf_op jit(solution)/shard_map/psum | solution.py:137
  945.5 85.7 %all_to_all.10 = f32[64,16,3,256]{3,1,2,0:T(8,128)S(1)} all-to-all(f32[64,16,3,256]{3,1,2,0:T(8,128)S(1)} %stack.460), channel_id=1, replica_groups=mesh['det'=64,'tm'=4] {'det'}, dimensions={0} | all-to-all | bytes 6291456 | tf_op jit(solution)/shard_map/all_to_all | solution.py:166
  1034.3 2.1 collective-permute-start.2
  1037.8 2.9 collective-permute-done.3
  1042.2 2.1 fusion.16
  1044.4 3.3 reshape.872
  1049.6 190.7 %all-reduce.12.cloned.1.call-done = f32[1024,3,256]{2,1,0:T(4,128)} async-done(((f32[1024,3,256]{2,1,0:T(4,128)}), f32[1024,3,256]{2,1,0:T(4,128)}) %all-reduce.12.cloned.1.call-update) | async-done | bytes 3145744
  1241.2 13.5 psum.51
  1255.4 130.2 %all-reduce.5 = (f32[]{:T(128)}, f32[]{:T(128)}) all-reduce(f32[]{:T(128)} %get-tuple-element.19, f32[]{:T(128)} %get-tuple-element.18), channel_id=1, replica_groups=mesh['det'=64,'tm'=4] {'det'}, use_global_device_ids=true, to_apply=%region_68.69 | all-reduce | flops 2 | bytes 16 | tf_op jit(solution)/shard_map/psum | solution.py:83
  1387.6 124.7 %psum.53 = f32[]{:T(128)} all-reduce(f32[]{:T(128)} %multiply_reduce_fusion.1), channel_id=1, replica_groups=mesh['det'=64,'tm'=4] {'det'}, use_global_device_ids=true, to_apply=%region_74.75 | all-reduce | flops 1 | bytes 8 | tf_op jit(solution)/shard_map/psum | solution.py:83
  1514.0 79.3 %all_to_all.11 = f32[64,16,3,256]{3,1,2,0:T(8,128)S(1)} all-to-all(f32[64,16,3,256]{3,1,2,0:T(8,128)S(1)} %stack.466), channel_id=1, replica_groups=mesh['det'=64,'tm'=4] {'det'}, dimensions={0} | all-to-all | bytes 6291456 | tf_op jit(solution)/shard_map/all_to_all | solution.py:166
  1599.2 2.9 collective-permute-done.5
  1603.7 2.1 fusion.14
  1605.8 3.3 reshape.878
  1609.1 191.5 %all-reduce.14.cloned.1.call-done = f32[1024,3,256]{2,1,0:T(4,128)} async-done(((f32[1024,3,256]{2,1,0:T(4,128)}), f32[1024,3,256]{2,1,0:T(4,128)}) %all-reduce.14.cloned.1.call-update) | async-done | bytes 3145744
  1801.5 13.5 psum.54
  1815.7 130.2 %psum.55 = f32[]{:T(128)} all-reduce(f32[]{:T(128)} %multiply_reduce_fusion), channel_id=1, replica_groups=mesh['det'=64,'tm'=4] {'det'}, use_global_device_ids=true, to_apply=%region_78.79 | all-reduce | flops 1 | bytes 8 | tf_op jit(solution)/shard_map/psum | solution.py:83
  (190 shorter events, 111.7 us)
Async XLA Ops:
  7.2 885.9 %reduce-scatter.2.cloned.1.call-start = ((), (), s32[]{:S(2)}) async-start(), calls=%async_computation.3 | async-start | bytes 9584640 | tf_op jit(solution)/shard_map/reduce_scatter | solution.py:136
  8.6 690.9 %collective-permute-start = (f32[1,64]{1,0:T(1,128)S(1)}, f32[1,64]{1,0:T(1,128)S(1)}, u32[]{:S(2)}, u32[]{:S(2)}) collective-permute-start(f32[1,64]{1,0:T(1,128)S(1)} %get-tuple-element.57), channel_id=1, source_target_pairs={{0,1},{1,2},{2,3},{4,5},{5,6},{6,7},{8,9},{9,10},{10,11},{12,13},{... | collective-permute-start | bytes 776 | tf_op jit(solution)/shard_map/ppermute | solution.py:25
  12.6 687.0 %collective-permute-start.1 = (f32[1,64]{1,0:T(1,128)S(1)}, f32[1,64]{1,0:T(1,128)S(1)}, u32[]{:S(2)}, u32[]{:S(2)}) collective-permute-start(f32[1,64]{1,0:T(1,128)S(1)} %get-tuple-element.56), channel_id=1, source_target_pairs={{1,0},{2,1},{3,2},{5,4},{6,5},{7,6},{9,8},{10,9},{11,10},{13,12},{... | collective-permute-start | bytes 776 | tf_op jit(solution)/shard_map/ppermute | solution.py:27
  113.3 584.0 %copy-start.3 = (f32[1,1,1024]{2,1,0:T(1,128)S(1)}, f32[1,1,1024]{2,1,0:T(1,128)}, u32[]{:S(2)}) copy-start(f32[1,1,1024]{2,1,0:T(1,128)} %param.11) | copy-start | bytes 12292
  113.3 584.7 %copy-start.6 = (s32[1,128]{1,0:T(1,128)S(1)}, s32[1,128]{1,0:T(1,128)}, u32[]{:S(2)}) copy-start(s32[1,128]{1,0:T(1,128)} %param.14) | copy-start | bytes 1540
  113.3 585.5 %copy-start.5 = (s32[1,1,1024]{2,1,0:T(1,128)S(1)}, s32[1,1,1024]{2,1,0:T(1,128)}, u32[]{:S(2)}) copy-start(s32[1,1,1024]{2,1,0:T(1,128)} %param.12) | copy-start | bytes 12292
  113.3 587.6 %copy-start.4 = (s32[1,1,4]{2,1,0:T(1,128)S(1)}, s32[1,1,4]{2,1,0:T(1,128)}, u32[]{:S(2)}) copy-start(s32[1,1,4]{2,1,0:T(1,128)} %param.13) | copy-start | bytes 52
  697.3 343.5 %copy-start.1 = (f32[1,384,256]{2,1,0:T(8,128)}, f32[1,384,256]{2,1,0:T(8,128)S(1)}, u32[]{:S(2)}) copy-start(f32[1,384,256]{2,1,0:T(8,128)S(1)} %reshape.880) | copy-start | bytes 1179652
  737.2 205.4 %all-reduce.10.cloned.1.call-start = ((), (), s32[]{:S(2)}) async-start(), calls=%async_computation.4 | async-start | bytes 294912 | tf_op jit(solution)/shard_map/psum | solution.py:137
  893.1 347.2 %all-reduce.12.cloned.1.call-start = ((), (), s32[]{:S(2)}) async-start(), calls=%async_computation.5 | async-start | bytes 8388608
  1034.3 3.4 collective-permute-start.2
  1036.3 4.3 collective-permute-start.3
  1047.6 0.7 copy-start.7
  1047.7 207.1 %copy-start = (f32[16,9,256]{2,0,1:T(8,128)S(1)}, f32[16,9,256]{2,0,1:T(8,128)}, u32[]{:S(2)}) copy-start(f32[16,9,256]{2,0,1:T(8,128)} %all-reduce.10.cloned.1.call-done) | copy-start | bytes 442372
  1047.7 752.9 %all-reduce.14.cloned.1.call-start = ((), (), s32[]{:S(2)}) async-start(), calls=%async_computation.6 | async-start | bytes 8388608
  1593.6 8.7 copy-start.2
  1596.5 2.6 collective-permute-start.4
  1597.8 4.3 collective-permute-start.5
Sparse Core Ops, SparseCore 0:
  737.3 155.7 reduce-scatter.1
  895.4 47.0 all-reduce.9
  1047.8 192.4 all-reduce.11
  1609.2 191.3 all-reduce.13
